TPU v7x, 256 devices: a whole 4x4x8 slice. The times are simulated.
256 devices in a mesh: pts: 64 (over z, x, core), cen: 4 (over y).
Axes of the slice: x: 4, y: 4, z: 8, core: 2. Of those that a mesh axis runs over, the one named last changes fastest.
Arguments:
- points: bfloat16 [131072, 768], P('pts'), may hold values from -16 to 16
- centroids: bfloat16 [4096, 768], P('cen'), may hold values from -1 to 1
Outputs:
- new_centroids: bfloat16 [4096, 768], P(('cen', 'pts'))
- distances: float32 [131072], P('pts')
All inputs are finite; a program needn't handle non-finite values.
Results may differ from a plain program's by a relative error of at most 0.0034.
Values may be sent and summed in bfloat16 or wider, within the bound.
No kernel may reach another device: no remote copies, remote signals or barrier semaphores. Data moves between devices by JAX's collectives and lax.ppermute only.
A program may use at most 64 MiB of HBM per device.

v0:
```python
import math
import jax
import jax.numpy as jnp
from jax import lax
from jax.sharding import PartitionSpec as P

ITERS = 3
sharpness = 4.0


def merged(value, axis, join):
    pieces = jax.tree.map(lambda part: lax.all_gather(part, axis), value)
    head = jax.tree.map(lambda part: part[0], pieces)
    tail = jax.tree.map(lambda part: part[1:], pieces)
    subtotal, _ = lax.scan(lambda subtotal, piece: (join(subtotal, piece), None), head, tail)
    return subtotal


def logits(points, centroids):
    product = lax.dot_general(
        points, centroids, (((1,), (1,)), ((), ())), preferred_element_type=jnp.float32
    )
    return sharpness * product


def combine_lse(earlier, later):
    joined_max = jnp.maximum(earlier[0], later[0])
    summed = earlier[1] * jnp.exp(earlier[0] - joined_max) + later[1] * jnp.exp(
        later[0] - joined_max
    )
    return (joined_max, summed)


def on_device(points, centroids):
    pts_devices = lax.axis_size("pts")
    total_points = points.shape[0] * pts_devices
    local_centroids = centroids.shape[0]
    total_centroids = local_centroids * lax.axis_size("cen")
    width = points.shape[1]
    stored_scores = logits(points, centroids)

    def current_scores():
        return stored_scores

    col_potential = jnp.zeros((local_centroids,), jnp.float32)
    row_potential = jnp.zeros((points.shape[0],), jnp.float32)
    for iteration in range(ITERS):
        shifted = current_scores() + col_potential[None, :]
        highest = jnp.max(shifted, axis=1)
        summed = jnp.sum(jnp.exp(shifted - highest[:, None]), axis=1)
        highest, summed = merged((highest, summed), "cen", combine_lse)
        row_potential = -math.log(total_points) - (highest + jnp.log(summed))
        shifted = current_scores() + row_potential[:, None]
        highest = lax.pmax(jnp.max(shifted, axis=0), "pts")
        summed = lax.psum(jnp.sum(jnp.exp(shifted - highest[None, :]), axis=0), "pts")
        col_potential = -math.log(total_centroids) - (highest + jnp.log(summed))
    transport = jnp.exp(current_scores() + row_potential[:, None] + col_potential[None, :])
    weights = transport.astype(jnp.bfloat16)
    rows_each = local_centroids // pts_devices
    product = lax.dot_general(
        weights, points, (((0,), (0,)), ((), ())), preferred_element_type=jnp.float32
    )
    partial_sums = total_centroids * product
    gathered_block = lax.psum(partial_sums, "pts").astype(jnp.bfloat16)
    own_rows = lax.dynamic_slice_in_dim(
        gathered_block, lax.axis_index("pts") * rows_each, rows_each, 0
    )
    block_float = gathered_block.astype(jnp.float32)
    squares = jnp.sum(block_float * block_float, axis=1)
    cross_terms = lax.dot_general(
        points, gathered_block, (((1,), (1,)), ((), ())), preferred_element_type=jnp.float32
    )
    numerator = jnp.sum(transport * (squares[None, :] - 2.0 * cross_terms), axis=1)
    row_mass = jnp.sum(transport, axis=1)
    numerator, row_mass = lax.psum((numerator, row_mass), "cen")
    distances = numerator / row_mass / width
    return (own_rows, distances)


def solution(mesh):
    in_specs = (P("pts", None), P("cen", None))
    out_specs = (P(("cen", "pts"), None), P("pts"))
    return jax.shard_map(
        on_device, mesh=mesh, in_specs=in_specs, out_specs=out_specs, check_vma=False
    )
```

profile of v0, /device:TPU:0, one launch (start us, length us, event | category | flops | bytes accessed | tf_op | source)
XLA Modules:
  0.0 1194.2 jit_solution(11087072551796998977)
XLA Ops:
  0.6 0.0 copy-start
  0.6 1.9 copy-done
  2.5 7.0 fusion.10
  9.6 11.9 all-gather
  21.5 4.6 exponential_reduce_fusion.5
  26.0 11.9 all-gather.1
  38.0 0.2 while.36
  38.2 4.0 add_reduce_fusion.3
  42.2 125.5 %pmax.21 = f32[1024]{0:T(1024)S(1)} all-reduce(f32[1024]{0:T(1024)S(1)} %add_reduce_fusion.3), channel_id=1, replica_groups=mesh['pts'=64,'cen'=4] {'pts'}, use_global_device_ids=true, to_apply=%region_5.6 | all-reduce | flops 1024 | bytes 8192 | tf_op jit(solution)/shard_map/pmax | solution.py:54
  167.7 4.4 exponential_reduce_fusion.4
  172.1 124.4 %psum.42 = f32[1024]{0:T(1024)S(1)} all-reduce(f32[1024]{0:T(1024)S(1)} %exponential_reduce_fusion.4), channel_id=1, replica_groups=mesh['pts'=64,'cen'=4] {'pts'}, use_global_device_ids=true, to_apply=%region_7.8 | all-reduce | flops 1024 | bytes 8192 | tf_op jit(solution)/shard_map/psum | solution.py:55
  296.5 4.0 add_reduce_fusion.2
  300.5 11.9 all-gather.2
  312.4 4.3 exponential_reduce_fusion.3
  316.7 11.9 all-gather.3
  328.7 0.2 while.37
  328.9 4.0 add_reduce_fusion.1
  332.9 124.1 %pmax.22 = f32[1024]{0:T(1024)S(1)} all-reduce(f32[1024]{0:T(1024)S(1)} %add_reduce_fusion.1), channel_id=1, replica_groups=mesh['pts'=64,'cen'=4] {'pts'}, use_global_device_ids=true, to_apply=%region_13.14 | all-reduce | flops 1024 | bytes 8192 | tf_op jit(solution)/shard_map/pmax | solution.py:54
  457.0 4.4 exponential_reduce_fusion.2
  461.3 124.1 %psum.43 = f32[1024]{0:T(1024)S(1)} all-reduce(f32[1024]{0:T(1024)S(1)} %exponential_reduce_fusion.2), channel_id=1, replica_groups=mesh['pts'=64,'cen'=4] {'pts'}, use_global_device_ids=true, to_apply=%region_15.16 | all-reduce | flops 1024 | bytes 8192 | tf_op jit(solution)/shard_map/psum | solution.py:55
  585.4 4.0 add_reduce_fusion
  589.4 11.9 all-gather.4
  601.3 4.3 exponential_reduce_fusion.1
  605.6 11.9 all-gather.5
  617.6 0.2 while.38
  617.8 4.0 add_reduce_fusion.4
  621.8 124.1 %pmax.23 = f32[1024]{0:T(1024)S(1)} all-reduce(f32[1024]{0:T(1024)S(1)} %add_reduce_fusion.4), channel_id=1, replica_groups=mesh['pts'=64,'cen'=4] {'pts'}, use_global_device_ids=true, to_apply=%region_21.22 | all-reduce | flops 1024 | bytes 8192 | tf_op jit(solution)/shard_map/pmax | solution.py:54
  745.9 4.4 exponential_reduce_fusion
  750.3 124.2 %psum.44 = f32[1024]{0:T(1024)S(1)} all-reduce(f32[1024]{0:T(1024)S(1)} %exponential_reduce_fusion), channel_id=1, replica_groups=mesh['pts'=64,'cen'=4] {'pts'}, use_global_device_ids=true, to_apply=%region_23.24 | all-reduce | flops 1024 | bytes 8192 | tf_op jit(solution)/shard_map/psum | solution.py:55
  874.5 8.8 fusion.7
  883.3 279.3 %all-reduce.2 = bf16[1024,768]{1,0:T(8,128)(2,1)} all-reduce(f32[1024,768]{1,0:T(8,128)} %fusion.7), channel_id=1, replica_groups=mesh['pts'=64,'cen'=4] {'pts'}, use_global_device_ids=true, to_apply=%region_24.25 | all-reduce | flops 786432 | bytes 4718592 | tf_op jit(solution)/shard_map/psum | solution.py:64
  1162.6 1.3 constant_dynamic-slice_fusion.6
  1163.9 1.8 multiply_reduce_fusion
  1165.7 6.9 fusion
  1172.6 4.3 fusion.1
  1176.9 16.6 %all-reduce = (f32[2048]{0:T(1024)S(1)}, f32[2048]{0:T(1024)S(1)}) all-reduce(f32[2048]{0:T(1024)S(1)} %fusion, f32[2048]{0:T(1024)S(1)} %fusion.1), channel_id=1, replica_groups=mesh['pts'=64,'cen'=4] {'cen'}, use_global_device_ids=true, to_apply=%region_27.28 | all-reduce | flops 4096 | bytes 32768 | tf_op jit(solution)/shard_map/psum | solution.py:75
  1193.5 0.6 divide_multiply_fusion
  (42 shorter events, 0.5 us)
Async XLA Ops:
  0.6 1.9 copy-start
where the time goes:
time: 1190 us
  blocking collectives  1110 us (93%)
  other arithmetic  53.1 us (4%)
  matrix products  22.7 us (2%)
    pmax x3, blocking collectives, on_device(): highest = lax.pmax(jnp.max(shifted, axis=0), 'pts')  374 us
    psum x3, blocking collectives, on_device(): lax.psum(jnp.sum(jnp.exp(shifted - highest[None, :]), axis=0), 'pts')  373 us
    psum x1, blocking collectives, on_device(): gathered_block = lax.psum(partial_sums, 'pts').astype(jnp.bfloat16)  279 us
    all_gather x6, blocking collectives, merged(): pieces = jax.tree.map(lambda part: lax.all_gather(part, axis), value)  71.5 us

commit v1 on v0

--- a/solution.py
+++ b/solution.py
@@ -52,7 +52,9 @@
         row_potential = -math.log(total_points) - (highest + jnp.log(summed))
         shifted = current_scores() + row_potential[:, None]
         highest = lax.pmax(jnp.max(shifted, axis=0), "pts")
-        summed = lax.psum(jnp.sum(jnp.exp(shifted - highest[None, :]), axis=0), "pts")
+        summed = jnp.sum(
+            lax.all_gather(jnp.sum(jnp.exp(shifted - highest[None, :]), axis=0), "pts"), axis=0
+        )
         col_potential = -math.log(total_centroids) - (highest + jnp.log(summed))
     transport = jnp.exp(current_scores() + row_potential[:, None] + col_potential[None, :])
     weights = transport.astype(jnp.bfloat16)

time: 1190 us -> 957 us (0.80)
  blocking collectives: 1110 us -> 871 us
    psum x3 -> x0, blocking collectives: 373 us -> none  [on_device(): lax.psum(jnp.sum(jnp.exp(shifted - highest[None, :]), axis=0), 'pts')]
    all_gather x0 -> x3, blocking collectives: none -> 126 us  [on_device(): lax.all_gather(jnp.sum(jnp.exp(shifted - highest[None, :]), axis=0), 'pts')]
where the time goes in v1:
time: 957 us; the launch traced here: 956 us
  blocking collectives  871 us (91%)
  other arithmetic  55.1 us (6%)
  matrix products  22.7 us (2%)
    pmax x3, blocking collectives, on_device(): highest = lax.pmax(jnp.max(shifted, axis=0), 'pts')  374 us
    psum x1, blocking collectives, on_device(): gathered_block = lax.psum(partial_sums, 'pts').astype(jnp.bfloat16)  283 us
    all_gather x3, blocking collectives, on_device(): lax.all_gather(jnp.sum(jnp.exp(shifted - highest[None, :]), axis=0), 'pts')  126 us
    all_gather x6, blocking collectives, merged(): pieces = jax.tree.map(lambda part: lax.all_gather(part, axis), value)  71.5 us

profile of v1, /device:TPU:0, one launch (start us, length us, event | category | flops | bytes accessed | tf_op | source)
XLA Modules:
  0.0 955.7 jit_solution(653687739994679006)
XLA Ops:
  0.6 0.0 copy-start
  0.6 1.9 copy-done
  2.5 7.0 fusion.10
  9.6 11.9 %all-gather = f32[8192]{0:T(1024)S(1)} all-gather(f32[2048]{0:T(1024)S(1)} %get-tuple-element.136), channel_id=2, replica_groups=mesh['pts'=64,'cen'=4] {'cen'}, dimensions={0}, use_global_device_ids=true | all-gather | bytes 40960 | tf_op jit(solution)/shard_map/all_gather | solution.py:12
  21.5 4.6 exponential_reduce_fusion.5
  26.0 11.9 %all-gather.1 = f32[8192]{0:T(1024)S(1)} all-gather(f32[2048]{0:T(1024)S(1)} %exponential_reduce_fusion.5), channel_id=3, replica_groups=mesh['pts'=64,'cen'=4] {'cen'}, dimensions={0}, use_global_device_ids=true | all-gather | bytes 40960 | tf_op jit(solution)/shard_map/all_gather | solution.py:12
  38.0 0.2 while.36
  38.2 4.0 add_reduce_fusion.3
  42.2 125.5 %pmax.21 = f32[1024]{0:T(1024)S(1)} all-reduce(f32[1024]{0:T(1024)S(1)} %add_reduce_fusion.3), channel_id=1, replica_groups=mesh['pts'=64,'cen'=4] {'pts'}, use_global_device_ids=true, to_apply=%region_5.6 | all-reduce | flops 1024 | bytes 8192 | tf_op jit(solution)/shard_map/pmax | solution.py:54
  167.7 4.4 exponential_reduce_fusion.4
  172.1 41.0 %all-gather.2 = f32[65536]{0:T(1024)S(1)} all-gather(f32[1024]{0:T(1024)S(1)} %exponential_reduce_fusion.4), channel_id=4, replica_groups=mesh['pts'=64,'cen'=4] {'pts'}, dimensions={0}, use_global_device_ids=true | all-gather | bytes 266240 | tf_op jit(solution)/shard_map/all_gather | solution.py:56
  213.1 0.8 reshape.19
  213.8 1.0 reduce_sum.110
  214.8 4.0 add_reduce_fusion.2
  218.8 11.9 %all-gather.3 = f32[8192]{0:T(1024)S(1)} all-gather(f32[2048]{0:T(1024)S(1)} %add_reduce_fusion.2), channel_id=5, replica_groups=mesh['pts'=64,'cen'=4] {'cen'}, dimensions={0}, use_global_device_ids=true | all-gather | bytes 40960 | tf_op jit(solution)/shard_map/all_gather | solution.py:12
  230.7 4.3 exponential_reduce_fusion.3
  235.1 11.9 %all-gather.4 = f32[8192]{0:T(1024)S(1)} all-gather(f32[2048]{0:T(1024)S(1)} %exponential_reduce_fusion.3), channel_id=6, replica_groups=mesh['pts'=64,'cen'=4] {'cen'}, dimensions={0}, use_global_device_ids=true | all-gather | bytes 40960 | tf_op jit(solution)/shard_map/all_gather | solution.py:12
  247.0 0.2 while.37
  247.2 4.0 add_reduce_fusion.1
  251.2 124.1 %pmax.22 = f32[1024]{0:T(1024)S(1)} all-reduce(f32[1024]{0:T(1024)S(1)} %add_reduce_fusion.1), channel_id=1, replica_groups=mesh['pts'=64,'cen'=4] {'pts'}, use_global_device_ids=true, to_apply=%region_13.14 | all-reduce | flops 1024 | bytes 8192 | tf_op jit(solution)/shard_map/pmax | solution.py:54
  375.3 4.4 exponential_reduce_fusion.2
  379.7 41.2 %all-gather.5 = f32[65536]{0:T(1024)S(1)} all-gather(f32[1024]{0:T(1024)S(1)} %exponential_reduce_fusion.2), channel_id=7, replica_groups=mesh['pts'=64,'cen'=4] {'pts'}, dimensions={0}, use_global_device_ids=true | all-gather | bytes 266240 | tf_op jit(solution)/shard_map/all_gather | solution.py:56
  420.8 0.8 reshape.22
  421.6 1.0 reduce_sum.113
  422.6 4.0 add_reduce_fusion
  426.6 11.9 %all-gather.6 = f32[8192]{0:T(1024)S(1)} all-gather(f32[2048]{0:T(1024)S(1)} %add_reduce_fusion), channel_id=8, replica_groups=mesh['pts'=64,'cen'=4] {'cen'}, dimensions={0}, use_global_device_ids=true | all-gather | bytes 40960 | tf_op jit(solution)/shard_map/all_gather | solution.py:12
  438.5 4.3 exponential_reduce_fusion.1
  442.8 11.9 %all-gather.7 = f32[8192]{0:T(1024)S(1)} all-gather(f32[2048]{0:T(1024)S(1)} %exponential_reduce_fusion.1), channel_id=9, replica_groups=mesh['pts'=64,'cen'=4] {'cen'}, dimensions={0}, use_global_device_ids=true | all-gather | bytes 40960 | tf_op jit(solution)/shard_map/all_gather | solution.py:12
  454.8 0.2 while.38
  455.0 4.0 add_reduce_fusion.4
  459.0 124.1 %pmax.23 = f32[1024]{0:T(1024)S(1)} all-reduce(f32[1024]{0:T(1024)S(1)} %add_reduce_fusion.4), channel_id=1, replica_groups=mesh['pts'=64,'cen'=4] {'pts'}, use_global_device_ids=true, to_apply=%region_21.22 | all-reduce | flops 1024 | bytes 8192 | tf_op jit(solution)/shard_map/pmax | solution.py:54
  583.1 4.4 exponential_reduce_fusion
  587.4 44.3 %all-gather.8 = f32[65536]{0:T(1024)} all-gather(f32[1024]{0:T(1024)S(1)} %exponential_reduce_fusion), channel_id=10, replica_groups=mesh['pts'=64,'cen'=4] {'pts'}, dimensions={0}, use_global_device_ids=true | all-gather | bytes 266240 | tf_op jit(solution)/shard_map/all_gather | solution.py:56
  631.7 1.0 reshape.25
  632.8 8.8 fusion.7
  641.6 282.5 %all-reduce.2 = bf16[1024,768]{1,0:T(8,128)(2,1)} all-reduce(f32[1024,768]{1,0:T(8,128)} %fusion.7), channel_id=1, replica_groups=mesh['pts'=64,'cen'=4] {'pts'}, use_global_device_ids=true, to_apply=%region_24.25 | all-reduce | flops 786432 | bytes 4718592 | tf_op jit(solution)/shard_map/psum | solution.py:66
  924.1 1.3 constant_dynamic-slice_fusion.6
  925.4 1.8 multiply_reduce_fusion
  927.2 6.9 fusion
  934.1 4.3 fusion.1
  938.4 16.6 %all-reduce = (f32[2048]{0:T(1024)S(1)}, f32[2048]{0:T(1024)S(1)}) all-reduce(f32[2048]{0:T(1024)S(1)} %fusion, f32[2048]{0:T(1024)S(1)} %fusion.1), channel_id=1, replica_groups=mesh['pts'=64,'cen'=4] {'cen'}, use_global_device_ids=true, to_apply=%region_27.28 | all-reduce | flops 4096 | bytes 32768 | tf_op jit(solution)/shard_map/psum | solution.py:77
  955.1 0.6 divide_multiply_fusion
  (43 shorter events, 0.5 us)
Async XLA Ops:
  0.6 1.9 copy-start
